TPU v7x, 128 devices: a whole 4x4x4 slice. The times are simulated.
128 devices in a mesh: board: 32 (over x, y, core), hand: 4 (over z).
Axes of the slice: x: 4, y: 4, z: 4, core: 2. Of those that a mesh axis runs over, the one named last changes fastest.
Arguments:
- reach_pre: float32 [1408], P(('board', 'hand')), may hold values from 0.05 to 1
- strategy: bfloat16 [256, 128, 1408], P('board', None, 'hand'), may hold values from 0 to 1
- ranks: int32 [256, 8, 1408], P('board'), may hold values from 0 to 94
- boards: int32 [256, 8, 5], P('board'), may hold values from 0 to 51, as said below
- river_live: int32 [256], P('board'), may hold values from 1 to 8, as said below
- iso_weight: int32 [256], P('board'), may hold values from 1 to 24
- pot: float32 [128], replicated, may hold values from 2 to 24
- line_act: int32 [128], replicated, may hold values from 0 to 2
Outputs:
- preflop_value: float32 [1408], P('hand')
Inputs may be any that keep to these rules, and one draw needn't show every extreme that they name: `boards`: the five cards of a runout are distinct; all runouts of a flop share their first three cards. `river_live`: in every draw some flop has all 8 runouts live.
All inputs are finite; a program needn't handle non-finite values.
Results may differ from a plain program's by a relative error of at most 0.0003.
Values may be sent and summed in bfloat16 or wider, within the bound.
A program may use at most 64 MiB of HBM per device.

v0:
```python
import jax
import jax.numpy as jnp
import numpy as np
from jax import lax
from jax.sharding import PartitionSpec as P

HANDS = 1326
HPAD = 1408
ACTS = 3


def card_tables():
    first_card, second_card = np.triu_indices(52, 1)
    padding = HPAD - HANDS
    first_card = np.concatenate([first_card, np.full(padding, 52)]).astype(np.int32)
    second_card = np.concatenate([second_card, np.full(padding, 53)]).astype(np.int32)
    alive_mask = np.concatenate([np.ones(HANDS), np.zeros(padding)]).astype(np.float32)
    return (jnp.asarray(first_card), jnp.asarray(second_card), jnp.asarray(alive_mask))


def unblocked(first_rows, second_rows, first_cols, second_cols):
    clear = (first_rows[:, None] != first_cols[None, :]) & (
        first_rows[:, None] != second_cols[None, :]
    )
    clear = (
        clear
        & (second_rows[:, None] != first_cols[None, :])
        & (second_rows[:, None] != second_cols[None, :])
    )
    return clear.astype(jnp.float32)


def live_hands(first_card, second_card, alive_mask, board_cards):
    clear = jnp.all(
        (first_card[:, None] != board_cards[None, :])
        & (second_card[:, None] != board_cards[None, :]),
        axis=1,
    )
    return alive_mask * clear.astype(jnp.float32)


def showdown(rank_rows, rank_cols, live_rows, live_cols, blocking):
    signed = jnp.sign(rank_rows[:, None] - rank_cols[None, :]).astype(jnp.float32)
    return (signed * blocking.astype(jnp.float32) * live_rows[:, None] * live_cols[None, :]).astype(
        jnp.bfloat16
    )


def runout_sum(
    ranks_flop, boards_flop, count_flop, tables, row_span, col_span, blocking, reach_flop
):
    first_card, second_card, alive_mask = tables
    row_start, row_len = row_span
    col_start, col_len = col_span

    def add_runout(runout, acc, factor):
        rank_now = ranks_flop[runout]
        live_now = live_hands(first_card, second_card, alive_mask, boards_flop[runout])
        matrix = showdown(
            lax.dynamic_slice_in_dim(rank_now, row_start, row_len),
            rank_now,
            lax.dynamic_slice_in_dim(live_now, row_start, row_len),
            lax.dynamic_slice_in_dim(live_now, col_start, col_len),
            blocking,
        )
        values = lax.dot_general(
            matrix, reach_flop, (((1,), (1,)), ((), ())), preferred_element_type=jnp.float32
        )
        return acc + values * factor

    empty = jnp.zeros((row_len, reach_flop.shape[0]), jnp.float32)

    def every_step(runout, acc):
        return add_runout(runout, acc, (runout < count_flop).astype(jnp.float32))

    return lax.fori_loop(0, ranks_flop.shape[0], every_step, empty)


def body(reach_pre, strategy, ranks, boards, river_live, iso_weight, pot, line_act):
    tables = card_tables()
    first_card, second_card, alive_mask = tables
    full_reach = lax.all_gather(reach_pre, ("board", "hand"), axis=0, tiled=True)
    local_weight = jnp.sum(iso_weight.astype(jnp.float32))
    weight_total = lax.psum(local_weight, "board")
    total_reach = jnp.sum(full_reach * alive_mask)
    hand_rows = strategy.shape[2]
    slots = full_reach.shape[0]
    row_start = lax.axis_index("hand") * hand_rows
    own_first = lax.dynamic_slice_in_dim(first_card, row_start, hand_rows)
    own_second = lax.dynamic_slice_in_dim(second_card, row_start, hand_rows)
    own_reach = lax.dynamic_slice_in_dim(full_reach, row_start, hand_rows)
    line_reach = (own_reach[None, None, :] * strategy.astype(jnp.float32) / total_reach).astype(
        jnp.bfloat16
    )
    onehot = (line_act[:, None] == jnp.arange(ACTS, dtype=jnp.int32)[None, :]).astype(jnp.float32)
    flop_ids = jnp.arange(strategy.shape[0], dtype=jnp.int32)
    every_reach = lax.all_gather(line_reach, "hand", axis=2, tiled=True)
    blocking = unblocked(own_first, own_second, first_card, second_card).astype(jnp.bfloat16)

    def own_rows(flop_index):
        return runout_sum(
            ranks[flop_index],
            boards[flop_index],
            river_live[flop_index],
            tables,
            (row_start, hand_rows),
            (0, slots),
            blocking,
            every_reach[flop_index],
        )

    acc = lax.map(own_rows, flop_ids)
    line_values = acc * pot[None, None, :] / river_live.astype(jnp.float32)[:, None, None]
    group_values = jnp.dot(
        line_values, onehot, precision=lax.Precision.HIGHEST, preferred_element_type=jnp.float32
    )
    best = jnp.max(group_values, axis=2)
    partial_values = jnp.sum(iso_weight.astype(jnp.float32)[:, None] * best, axis=0)
    summed = lax.psum(partial_values, "board")
    return summed / weight_total


def solution(mesh):
    in_specs = (
        P(("board", "hand")),
        P("board", None, "hand"),
        P("board", None, None),
        P("board", None, None),
        P("board"),
        P("board"),
        P(),
        P(),
    )
    out_specs = P("hand")
    return jax.shard_map(body, mesh=mesh, in_specs=in_specs, out_specs=out_specs, check_vma=False)
```

profile of v0, /device:TPU:0, one launch (start us, length us, event | category | flops | bytes accessed | tf_op | source)
XLA Modules:
  0.0 370.8 jit_solution(5847999569311250122)
XLA Ops:
  7.5 68.2 %all-reduce = f32[1408]{0:T(1024)S(1)} all-reduce(f32[1408]{0:T(1024)S(1)} %dynamic-update-slice), channel_id=1, replica_groups=mesh['board'=32,'hand'=4] {'board','hand'}, use_global_device_ids=true, to_apply=%add | all-reduce | flops 1408 | bytes 11264
  75.8 1.3 multiply_reduce_fusion.1
  77.1 3.0 divide_convert_fusion
  80.9 33.0 %all-gather.2.cloned.1.call-done = bf16[8,128,1408]{1,0,2:T(8,128)(2,1)} async-done(((bf16[8,128,352]{1,0,2:T(8,128)(2,1)}), bf16[8,128,1408]{1,0,2:T(8,128)(2,1)}) %all-gather.2.cloned.1.call-update) | async-done | bytes 2883600 | tf_op jit(solution)/shard_map/all_gather | solution.py:97
  114.0 4.8 %copy.19 = bf16[8,128,1408]{2,1,0:T(8,128)(2,1)} copy(bf16[8,128,1408]{1,0,2:T(8,128)(2,1)} %all-gather.2.cloned.1.call-done) | data formatting | bytes 5767168
  118.8 175.5 %while.50 = (s32[]{:T(128)}, f32[8,352,128]{2,1,0:T(8,128)S(1)}, s32[8]{0:T(128)S(1)}, s32[8]{0:T(128)S(1)}, s32[8,8,1408]{2,1,0:T(8,128)}, /*index=5*/s32[8,8,5...) while((s32[]{:T(128)}, f32[8,352,128]{2,1,0:T(8,128)S(1)}, ...), condition=%wide.region_5.6_spmd.clone.clone, body=%wide.region_1.5_spmd.sunk.clone.clone.sunk | while | flops 135466512 | bytes 3946544 | solution.py:112
  121.5 1.0 dynamic-slice_bitcast_fusion.7
  125.5 15.2 %while.51 = (s32[]{:T(128)}, f32[352,128]{1,0:T(8,128)S(1)}, s32[8,1408]{1,0:T(8,128)S(1)}, s32[]{:T(128)}, bf16[352,1408]{1,0:T(8,128)(2,1)S(1)}, /*index=5*/s3...) while((s32[]{:T(128)}, f32[352,128]{1,0:T(8,128)S(1)}, ...), condition=%wide.region_4.4_spmd.clone.clone, body=%wide.region_2.0_spmd.sunk.clone.clone.sunk | while | flops 131005960 | bytes 1768713 | solution.py:76
  143.4 1.0 dynamic-slice_bitcast_fusion.7
  147.4 15.2 %while.51 = (s32[]{:T(128)}, f32[352,128]{1,0:T(8,128)S(1)}, s32[8,1408]{1,0:T(8,128)S(1)}, s32[]{:T(128)}, bf16[352,1408]{1,0:T(8,128)(2,1)S(1)}, /*index=5*/s3...) while((s32[]{:T(128)}, f32[352,128]{1,0:T(8,128)S(1)}, ...), condition=%wide.region_4.4_spmd.clone.clone, body=%wide.region_2.0_spmd.sunk.clone.clone.sunk | while | flops 131005960 | bytes 1768713 | solution.py:76
  150.3 0.9 fusion.17
  156.1 0.9 fusion.17
  161.8 0.9 fusion.17
  165.4 1.0 dynamic-slice_bitcast_fusion.7
  169.4 15.2 %while.51 = (s32[]{:T(128)}, f32[352,128]{1,0:T(8,128)S(1)}, s32[8,1408]{1,0:T(8,128)S(1)}, s32[]{:T(128)}, bf16[352,1408]{1,0:T(8,128)(2,1)S(1)}, /*index=5*/s3...) while((s32[]{:T(128)}, f32[352,128]{1,0:T(8,128)S(1)}, ...), condition=%wide.region_4.4_spmd.clone.clone, body=%wide.region_2.0_spmd.sunk.clone.clone.sunk | while | flops 131005960 | bytes 1768713 | solution.py:76
  172.3 0.9 fusion.17
  178.0 0.9 fusion.17
  187.3 1.0 dynamic-slice_bitcast_fusion.7
  191.3 15.2 %while.51 = (s32[]{:T(128)}, f32[352,128]{1,0:T(8,128)S(1)}, s32[8,1408]{1,0:T(8,128)S(1)}, s32[]{:T(128)}, bf16[352,1408]{1,0:T(8,128)(2,1)S(1)}, /*index=5*/s3...) while((s32[]{:T(128)}, f32[352,128]{1,0:T(8,128)S(1)}, ...), condition=%wide.region_4.4_spmd.clone.clone, body=%wide.region_2.0_spmd.sunk.clone.clone.sunk | while | flops 131005960 | bytes 1768713 | solution.py:76
  209.3 1.0 dynamic-slice_bitcast_fusion.7
  213.2 15.2 %while.51 = (s32[]{:T(128)}, f32[352,128]{1,0:T(8,128)S(1)}, s32[8,1408]{1,0:T(8,128)S(1)}, s32[]{:T(128)}, bf16[352,1408]{1,0:T(8,128)(2,1)S(1)}, /*index=5*/s3...) while((s32[]{:T(128)}, f32[352,128]{1,0:T(8,128)S(1)}, ...), condition=%wide.region_4.4_spmd.clone.clone, body=%wide.region_2.0_spmd.sunk.clone.clone.sunk | while | flops 131005960 | bytes 1768713 | solution.py:76
  231.2 1.0 dynamic-slice_bitcast_fusion.7
  235.2 15.2 %while.51 = (s32[]{:T(128)}, f32[352,128]{1,0:T(8,128)S(1)}, s32[8,1408]{1,0:T(8,128)S(1)}, s32[]{:T(128)}, bf16[352,1408]{1,0:T(8,128)(2,1)S(1)}, /*index=5*/s3...) while((s32[]{:T(128)}, f32[352,128]{1,0:T(8,128)S(1)}, ...), condition=%wide.region_4.4_spmd.clone.clone, body=%wide.region_2.0_spmd.sunk.clone.clone.sunk | while | flops 131005960 | bytes 1768713 | solution.py:76
  247.6 0.9 fusion.17
  253.1 1.0 dynamic-slice_bitcast_fusion.7
  257.1 15.2 %while.51 = (s32[]{:T(128)}, f32[352,128]{1,0:T(8,128)S(1)}, s32[8,1408]{1,0:T(8,128)S(1)}, s32[]{:T(128)}, bf16[352,1408]{1,0:T(8,128)(2,1)S(1)}, /*index=5*/s3...) while((s32[]{:T(128)}, f32[352,128]{1,0:T(8,128)S(1)}, ...), condition=%wide.region_4.4_spmd.clone.clone, body=%wide.region_2.0_spmd.sunk.clone.clone.sunk | while | flops 131005960 | bytes 1768713 | solution.py:76
  258.1 0.9 fusion.17
  275.1 1.0 dynamic-slice_bitcast_fusion.7
  279.0 15.2 %while.51 = (s32[]{:T(128)}, f32[352,128]{1,0:T(8,128)S(1)}, s32[8,1408]{1,0:T(8,128)S(1)}, s32[]{:T(128)}, bf16[352,1408]{1,0:T(8,128)(2,1)S(1)}, /*index=5*/s3...) while((s32[]{:T(128)}, f32[352,128]{1,0:T(8,128)S(1)}, ...), condition=%wide.region_4.4_spmd.clone.clone, body=%wide.region_2.0_spmd.sunk.clone.clone.sunk | while | flops 131005960 | bytes 1768713 | solution.py:76
  294.3 1.1 fusion.7
  295.5 67.3 %all-reduce.1 = (f32[352]{0:T(512)S(1)}, f32[]{:T(128)}) all-reduce(f32[352]{0:T(512)S(1)} %multiply_reduce_fusion, f32[]{:T(128)} %convert_reduce_fusion), channel_id=1, replica_groups=mesh['board'=32,'hand'=4] {'board'}, use_global_device_ids=true, to_apply=%region_8.9 | all-reduce | flops 353 | bytes 2824 | tf_op jit(solution)/shard_map/psum | solution.py:119
  362.8 1.1 broadcast_divide_fusion
  (532 shorter events, 100.9 us)
Async XLA Ops:
  6.5 73.6 %copy-start = (s32[1408]{0:T(1024)S(1)}, s32[1408]{0:T(1024)}, u32[]{:S(2)}) copy-start(s32[1408]{0:T(1024)} %constant.188.clone) | copy-start | bytes 16900
  6.5 73.7 %copy-start.1 = (s32[1408]{0:T(1024)S(1)}, s32[1408]{0:T(1024)}, u32[]{:S(2)}) copy-start(s32[1408]{0:T(1024)} %constant.189.clone) | copy-start | bytes 16900
  6.5 73.8 %copy-start.4 = (s32[8]{0:T(128)S(1)}, s32[8]{0:T(128)}, u32[]{:S(2)}) copy-start(s32[8]{0:T(128)} %param.19) | copy-start | bytes 100
  6.5 73.8 %copy-start.3 = (s32[8]{0:T(128)S(1)}, s32[8]{0:T(128)}, u32[]{:S(2)}) copy-start(s32[8]{0:T(128)} %param.20) | copy-start | bytes 100
  6.5 107.4 %all-gather.2.cloned.1.call-start = ((), (), s32[]{:S(2)}) async-start(), calls=%async_computation | async-start | bytes 3604480 | tf_op jit(solution)/shard_map/all_gather | solution.py:97
  80.9 37.9 %copy-start.2 = (f32[1408]{0:T(1024)S(1)}, f32[1408]{0:T(1024)}, u32[]{:S(2)}) copy-start(f32[1408]{0:T(1024)} %constant.190.clone) | copy-start | bytes 16900
  118.8 175.5 %copy-start.5 = (f32[128]{0:T(128)S(1)}, f32[128]{0:T(128)}, u32[]{:S(2)}) copy-start(f32[128]{0:T(128)} %param.21) | copy-start | bytes 1540
  118.8 175.5 %copy-start.6 = (s32[128]{0:T(128)S(1)}, s32[128]{0:T(128)}, u32[]{:S(2)}) copy-start(s32[128]{0:T(128)} %param.22) | copy-start | bytes 1540
Sparse Core Ops, SparseCore 0:
  80.3 33.6 all-gather.1
where the time goes:
time: 373 us; the launch traced here: 371 us
  blocking collectives  136 us (36%)
  loops' own time  62.2 us (17%)
  matrix products  57.1 us (15%)
  local copies, waits for them, and re-layouts  50.9 us (14%)
  waiting for transfers between devices  33 us (9%)
  other arithmetic  18.5 us (5%)
  between operations  13.5 us (4%)
    unnamed x1, blocking collectives  68.2 us
    psum x1, blocking collectives, body(): summed = lax.psum(partial_values, 'board')  67.3 us
    dot_general x64, matrix products, add_runout(): lax.dot_general(matrix, reach_flop, (((1,), (1,)), ((), ())), preferred_e...  56 us
    another operation x8, loops' own time, runout_sum(): return lax.fori_loop(0, ranks_flop.shape[0], every_step, empty)  45.6 us
    all_gather x1, waiting for transfers between devices, body(): every_reach = lax.all_gather(line_reach, 'hand', axis=2, tiled=True)  33 us
    another operation x1, loops' own time, body(): acc = lax.map(own_rows, flop_ids)  16.6 us
    squeeze x8, local copies, waits for them, and re-layouts, own_rows(): every_reach[flop_index]  8.15 us
  transfers between devices with their start and end apart: 1, of which 1 were waited for; matrix products, arithmetic and copies ran while one was open for 0% of the time, Pallas kernels for 0%

commit v1 on v0

--- a/solution.py
+++ b/solution.py
@@ -116,7 +116,17 @@
     )
     best = jnp.max(group_values, axis=2)
     partial_values = jnp.sum(iso_weight.astype(jnp.float32)[:, None] * best, axis=0)
-    summed = lax.psum(partial_values, "board")
+
+    def feed_ends(field_in, chip_axis="board"):
+        devs = lax.axis_size(chip_axis)
+        carry_out = field_in
+        for dd in [
+            [(ii, ii ^ num) for ii in range(devs)] for num in (1, 2, 4, 8, 16) if num < devs
+        ]:
+            carry_out = carry_out + lax.ppermute(carry_out, chip_axis, dd)
+        return carry_out
+
+    summed = feed_ends(partial_values)
     return summed / weight_total
 
 

time: 373 us -> 387 us (1.038)
  starting transfers between devices: 0.03 us -> 9.08 us
  waiting for transfers between devices: 33 us -> 41.1 us
  blocking collectives: 136 us -> 132 us
    ppermute x0 -> x5, starting transfers between devices: none -> 9.05 us  [feed_ends(): carry_out = carry_out + lax.ppermute(carry_out, chip_axis, dd)]
    ppermute x0 -> x5, waiting for transfers between devices: none -> 7.43 us  [feed_ends(): carry_out = carry_out + lax.ppermute(carry_out, chip_axis, dd)]
    psum x1, blocking collectives: 67.3 us -> 63.4 us  [body(): weight_total = lax.psum(local_weight, 'board')]
  transfers between devices with their start and end apart: 1 -> 6, of which waited for: 1 -> 5; matrix products, arithmetic and copies ran while one was open for 0% -> 0% of each run, Pallas kernels for 0% -> 0%
where the time goes in v1:
time: 387 us; the launch traced here: 384 us
  blocking collectives  132 us (34%)
  loops' own time  62.2 us (16%)
  matrix products  57.1 us (15%)
  local copies, waits for them, and re-layouts  50.9 us (13%)
  waiting for transfers between devices  41.1 us (11%)
  other arithmetic  18.7 us (5%)
  between operations  13.5 us (3%)
  starting transfers between devices  9.08 us (2%)
    unnamed x1, blocking collectives  68.2 us
    psum x1, blocking collectives, body(): weight_total = lax.psum(local_weight, 'board')  63.4 us
    dot_general x64, matrix products, add_runout(): lax.dot_general(matrix, reach_flop, (((1,), (1,)), ((), ())), preferred_e...  56 us
    another operation x8, loops' own time, runout_sum(): return lax.fori_loop(0, ranks_flop.shape[0], every_step, empty)  45.6 us
    all_gather x1, waiting for transfers between devices, body(): every_reach = lax.all_gather(line_reach, 'hand', axis=2, tiled=True)  33.6 us
    another operation x1, loops' own time, body(): acc = lax.map(own_rows, flop_ids)  16.6 us
    ppermute x5, starting transfers between devices, feed_ends(): carry_out = carry_out + lax.ppermute(carry_out, chip_axis, dd)  9.05 us
    squeeze x8, local copies, waits for them, and re-layouts, own_rows(): every_reach[flop_index]  8.15 us
  transfers between devices with their start and end apart: 6, of which 5 were waited for; matrix products, arithmetic and copies ran while one was open for 0% of the time, Pallas kernels for 0%

profile of v1, /device:TPU:0, one launch (start us, length us, event | category | flops | bytes accessed | tf_op | source)
XLA Modules:
  0.0 384.1 jit_solution(13361338037906738749)
XLA Ops:
  7.5 68.2 %all-reduce = f32[1408]{0:T(1024)S(1)} all-reduce(f32[1408]{0:T(1024)S(1)} %dynamic-update-slice), channel_id=1, replica_groups=mesh['board'=32,'hand'=4] {'board','hand'}, use_global_device_ids=true, to_apply=%add | all-reduce | flops 1408 | bytes 11264
  75.8 1.3 multiply_reduce_fusion.1
  77.1 3.0 divide_convert_fusion
  80.4 33.6 %all-gather.2.cloned.1.call-done = bf16[8,128,1408]{1,0,2:T(8,128)(2,1)} async-done(((bf16[8,128,352]{1,0,2:T(8,128)(2,1)}), bf16[8,128,1408]{1,0,2:T(8,128)(2,1)}) %all-gather.2.cloned.1.call-update) | async-done | bytes 2883600 | tf_op jit(solution)/shard_map/all_gather | solution.py:97
  114.0 4.8 %copy.19 = bf16[8,128,1408]{2,1,0:T(8,128)(2,1)} copy(bf16[8,128,1408]{1,0,2:T(8,128)(2,1)} %all-gather.2.cloned.1.call-done) | data formatting | bytes 5767168
  118.8 175.5 %while.50 = (s32[]{:T(128)}, f32[8,352,128]{2,1,0:T(8,128)S(1)}, s32[8]{0:T(128)S(1)}, s32[8]{0:T(128)S(1)}, s32[8,8,1408]{2,1,0:T(8,128)}, /*index=5*/s32[8,8,5...) while((s32[]{:T(128)}, f32[8,352,128]{2,1,0:T(8,128)S(1)}, ...), condition=%wide.region_5.6_spmd.clone.clone, body=%wide.region_1.5_spmd.sunk.clone.clone.sunk | while | flops 135466512 | bytes 3946544 | solution.py:112
  121.5 1.0 dynamic-slice_bitcast_fusion.7
  125.5 15.2 %while.51 = (s32[]{:T(128)}, f32[352,128]{1,0:T(8,128)S(1)}, s32[8,1408]{1,0:T(8,128)S(1)}, s32[]{:T(128)}, bf16[352,1408]{1,0:T(8,128)(2,1)S(1)}, /*index=5*/s3...) while((s32[]{:T(128)}, f32[352,128]{1,0:T(8,128)S(1)}, ...), condition=%wide.region_4.4_spmd.clone.clone, body=%wide.region_2.0_spmd.sunk.clone.clone.sunk | while | flops 131005960 | bytes 1768713 | solution.py:76
  143.5 1.0 dynamic-slice_bitcast_fusion.7
  147.4 15.2 %while.51 = (s32[]{:T(128)}, f32[352,128]{1,0:T(8,128)S(1)}, s32[8,1408]{1,0:T(8,128)S(1)}, s32[]{:T(128)}, bf16[352,1408]{1,0:T(8,128)(2,1)S(1)}, /*index=5*/s3...) while((s32[]{:T(128)}, f32[352,128]{1,0:T(8,128)S(1)}, ...), condition=%wide.region_4.4_spmd.clone.clone, body=%wide.region_2.0_spmd.sunk.clone.clone.sunk | while | flops 131005960 | bytes 1768713 | solution.py:76
  165.4 1.0 dynamic-slice_bitcast_fusion.7
  169.4 15.2 %while.51 = (s32[]{:T(128)}, f32[352,128]{1,0:T(8,128)S(1)}, s32[8,1408]{1,0:T(8,128)S(1)}, s32[]{:T(128)}, bf16[352,1408]{1,0:T(8,128)(2,1)S(1)}, /*index=5*/s3...) while((s32[]{:T(128)}, f32[352,128]{1,0:T(8,128)S(1)}, ...), condition=%wide.region_4.4_spmd.clone.clone, body=%wide.region_2.0_spmd.sunk.clone.clone.sunk | while | flops 131005960 | bytes 1768713 | solution.py:76
  187.3 1.0 dynamic-slice_bitcast_fusion.7
  191.3 15.2 %while.51 = (s32[]{:T(128)}, f32[352,128]{1,0:T(8,128)S(1)}, s32[8,1408]{1,0:T(8,128)S(1)}, s32[]{:T(128)}, bf16[352,1408]{1,0:T(8,128)(2,1)S(1)}, /*index=5*/s3...) while((s32[]{:T(128)}, f32[352,128]{1,0:T(8,128)S(1)}, ...), condition=%wide.region_4.4_spmd.clone.clone, body=%wide.region_2.0_spmd.sunk.clone.clone.sunk | while | flops 131005960 | bytes 1768713 | solution.py:76
  209.3 1.0 dynamic-slice_bitcast_fusion.7
  213.2 15.2 %while.51 = (s32[]{:T(128)}, f32[352,128]{1,0:T(8,128)S(1)}, s32[8,1408]{1,0:T(8,128)S(1)}, s32[]{:T(128)}, bf16[352,1408]{1,0:T(8,128)(2,1)S(1)}, /*index=5*/s3...) while((s32[]{:T(128)}, f32[352,128]{1,0:T(8,128)S(1)}, ...), condition=%wide.region_4.4_spmd.clone.clone, body=%wide.region_2.0_spmd.sunk.clone.clone.sunk | while | flops 131005960 | bytes 1768713 | solution.py:76
  231.2 1.0 dynamic-slice_bitcast_fusion.7
  235.2 15.2 %while.51 = (s32[]{:T(128)}, f32[352,128]{1,0:T(8,128)S(1)}, s32[8,1408]{1,0:T(8,128)S(1)}, s32[]{:T(128)}, bf16[352,1408]{1,0:T(8,128)(2,1)S(1)}, /*index=5*/s3...) while((s32[]{:T(128)}, f32[352,128]{1,0:T(8,128)S(1)}, ...), condition=%wide.region_4.4_spmd.clone.clone, body=%wide.region_2.0_spmd.sunk.clone.clone.sunk | while | flops 131005960 | bytes 1768713 | solution.py:76
  253.1 1.0 dynamic-slice_bitcast_fusion.7
  257.1 15.2 %while.51 = (s32[]{:T(128)}, f32[352,128]{1,0:T(8,128)S(1)}, s32[8,1408]{1,0:T(8,128)S(1)}, s32[]{:T(128)}, bf16[352,1408]{1,0:T(8,128)(2,1)S(1)}, /*index=5*/s3...) while((s32[]{:T(128)}, f32[352,128]{1,0:T(8,128)S(1)}, ...), condition=%wide.region_4.4_spmd.clone.clone, body=%wide.region_2.0_spmd.sunk.clone.clone.sunk | while | flops 131005960 | bytes 1768713 | solution.py:76
  279.0 15.2 %while.51 = (s32[]{:T(128)}, f32[352,128]{1,0:T(8,128)S(1)}, s32[8,1408]{1,0:T(8,128)S(1)}, s32[]{:T(128)}, bf16[352,1408]{1,0:T(8,128)(2,1)S(1)}, /*index=5*/s3...) while((s32[]{:T(128)}, f32[352,128]{1,0:T(8,128)S(1)}, ...), condition=%wide.region_4.4_spmd.clone.clone, body=%wide.region_2.0_spmd.sunk.clone.clone.sunk | while | flops 131005960 | bytes 1768713 | solution.py:76
  294.3 1.1 fusion.7
  295.6 1.1 collective-permute-done
  296.8 1.5 collective-permute-start.1
  298.3 2.1 collective-permute-done.1
  300.4 3.0 collective-permute-start.2
  303.4 2.1 collective-permute-done.2
  305.4 1.5 collective-permute-start.3
  306.9 2.1 collective-permute-done.3
  309.0 3.0 collective-permute-start.4
  312.6 63.4 %psum.7 = f32[]{:T(128)} all-reduce(f32[]{:T(128)} %convert_reduce_fusion), channel_id=1, replica_groups=mesh['board'=32,'hand'=4] {'board'}, use_global_device_ids=true, to_apply=%region_9.10 | all-reduce | flops 1 | bytes 8 | tf_op jit(solution)/shard_map/psum | solution.py:84
  376.0 1.3 add_divide_fusion
  (546 shorter events, 108.1 us)
Async XLA Ops:
  6.5 73.6 %copy-start = (s32[1408]{0:T(1024)S(1)}, s32[1408]{0:T(1024)}, u32[]{:S(2)}) copy-start(s32[1408]{0:T(1024)} %constant.188.clone) | copy-start | bytes 16900
  6.5 73.7 %copy-start.1 = (s32[1408]{0:T(1024)S(1)}, s32[1408]{0:T(1024)}, u32[]{:S(2)}) copy-start(s32[1408]{0:T(1024)} %constant.189.clone) | copy-start | bytes 16900
  6.5 73.8 %copy-start.3 = (s32[8]{0:T(128)S(1)}, s32[8]{0:T(128)}, u32[]{:S(2)}) copy-start(s32[8]{0:T(128)} %param.19) | copy-start | bytes 100
  6.5 73.8 %copy-start.6 = (s32[8]{0:T(128)S(1)}, s32[8]{0:T(128)}, u32[]{:S(2)}) copy-start(s32[8]{0:T(128)} %param.20) | copy-start | bytes 100
  6.5 107.4 %all-gather.2.cloned.1.call-start = ((), (), s32[]{:S(2)}) async-start(), calls=%async_computation | async-start | bytes 3604480 | tf_op jit(solution)/shard_map/all_gather | solution.py:97
  80.3 38.5 %copy-start.2 = (f32[1408]{0:T(1024)S(1)}, f32[1408]{0:T(1024)}, u32[]{:S(2)}) copy-start(f32[1408]{0:T(1024)} %constant.190.clone) | copy-start | bytes 16900
  118.8 175.5 %copy-start.4 = (f32[128]{0:T(128)S(1)}, f32[128]{0:T(128)}, u32[]{:S(2)}) copy-start(f32[128]{0:T(128)} %param.21) | copy-start | bytes 1540
  118.8 175.5 %copy-start.5 = (s32[128]{0:T(128)S(1)}, s32[128]{0:T(128)}, u32[]{:S(2)}) copy-start(s32[128]{0:T(128)} %param.22) | copy-start | bytes 1540
  295.5 1.2 collective-permute-start
  296.8 3.6 collective-permute-start.1
  300.4 5.1 %collective-permute-start.2 = (f32[352]{0:T(512)S(1)}, f32[352]{0:T(512)S(1)}, u32[]{:S(2)}, u32[]{:S(2)}) collective-permute-start(f32[352]{0:T(512)S(1)} %add.111), channel_id=1, source_target_pairs={{0,16},{4,20},{8,24},{12,28},{16,0},{20,4},{24,8},{28,12},{32,48},... | collective-permute-start | bytes 4232 | tf_op jit(solution)/shard_map/ppermute | solution.py:126
  305.4 3.6 collective-permute-start.3
  309.0 67.0 %collective-permute-start.4 = (f32[352]{0:T(512)S(1)}, f32[352]{0:T(512)S(1)}, u32[]{:S(2)}, u32[]{:S(2)}) collective-permute-start(f32[352]{0:T(512)S(1)} %add.113), channel_id=1, source_target_pairs={{0,64},{4,68},{8,72},{12,76},{16,80},{20,84},{24,88},{28,92},{32,9... | collective-permute-start | bytes 4232 | tf_op jit(solution)/shard_map/ppermute | solution.py:126
Sparse Core Ops, SparseCore 0:
  80.3 33.6 all-gather.1
